TPU v7x, 32 devices: a whole 2x2x4 slice. The times are simulated.
32 devices in a mesh: flow: 2 (over x), cross: 4 (over z), depth: 4 (over y, core).
Axes of the slice: x: 2, y: 2, z: 4, core: 2. Of those that a mesh axis runs over, the one named last changes fastest.
Arguments:
- fluid_offsets: float32 [3, 2, 16, 16, 128], P(None, 'flow', 'cross', 'depth'), may hold values from 0 to 1
- source: float32 [2, 16, 16, 128], P('flow', 'cross', 'depth'), may hold values from -6 to 6
- marker_offsets: float32 [512, 16, 3, 128], P(('flow', 'cross', 'depth')), may hold values from 0 to 1
- marker_normals: float32 [512, 16, 3, 128], P(('flow', 'cross', 'depth')), may hold values from -6 to 6
- dest_tile: int32 [512, 16, 1], P(('flow', 'cross', 'depth')), may hold values from 0 to 7; in each aligned block of 256 rows (0 to 255, 256 to 511, ..., all dimensions but the last counted through in order) at most 64 rows name the same one
- cell_index: int32 [512, 16], P(('flow', 'cross', 'depth')), may hold values from 0 to 15
- grain_velocity: float32 [512, 3], P(('flow', 'cross', 'depth')), may hold values from -6 to 6
- grain_mass: float32 [512], P(('flow', 'cross', 'depth')), may hold values from 0.5 to 4
Outputs:
- pressure: float32 [2, 16, 16, 128], P('flow', 'cross', 'depth')
- velocity_out: float32 [512, 3], P(('flow', 'cross', 'depth'))
Inputs may be any that keep to these rules, and one draw needn't show every extreme that they name: `dest_tile`: in the rows of one device at most 64 marker blocks name the same tile.
All inputs are finite; a program needn't handle non-finite values.
Results may differ from a plain program's by a relative error of at most 0.0003.
Values sent between devices are 32-bit elements; how exact they have to be, the bound alone decides.
A program may use at most 64 MiB of HBM per device.

v0:
```python
import functools
import math

import jax
import jax.numpy as jnp
from jax import lax
from jax.experimental import pallas as pl
from jax.experimental.pallas import tpu as pltpu
from jax.sharding import PartitionSpec as P

ITERS = 4
STEPS = 2
STIFFEN = 0.5
STEP_TIME = 0.05
PER_PARTICLE = 1.0 / 128.0
SCALE = math.sqrt(math.log2(math.e))
SHIFT = math.log2(PER_PARTICLE)
MESH = pl.DeviceIdType.MESH
HIGHEST = lax.Precision.HIGHEST
COLS = 8


def weight_of(gaps):
    total = None
    for gap in gaps:
        total = gap * gap if total is None else total + gap * gap
    return jnp.exp2(SHIFT - total)


def rounded(value):
    return value.astype(jnp.bfloat16).astype(jnp.float32)


def three_parts(value):
    high = rounded(value)
    middle = rounded(value - high)
    return high, middle, (value - high) - middle


def solve_small(gram, right):
    n = len(right)
    gram = [list(row) for row in gram]
    right = list(right)
    for i in range(n):
        inverse = 1.0 / gram[i][i]
        for j in range(i + 1, n):
            factor = gram[j][i] * inverse
            for k in range(i + 1, n):
                gram[j][k] = gram[j][k] - factor * gram[i][k]
            right[j] = right[j] - factor * right[i]
    out = [None] * n
    for i in reversed(range(n)):
        value = right[i]
        for k in range(i + 1, n):
            value = value - gram[i][k] * out[k]
        out[i] = value / gram[i][i]
    return out


def kernel(
    sizes,
    dims,
    slot_ref,
    cell_ref,
    off_ref,
    source_ref,
    geo_ref,
    start_ref,
    mass_ref,
    column_ref,
    row_ref,
    press_out,
    speed_out,
    off_group,
    off_depth,
    weights,
    geo_turned,
    own_features,
    shift_rows,
    normal_sums,
    give,
    take,
    krylov,
    krylov_depth,
    part_group,
    part_depth,
    off_send,
    off_recv,
    take_send,
    take_recv,
    kry_send,
    kry_recv,
    part_send,
    part_recv,
):
    n_flow, n_cross, n_depth = sizes
    size_x, size_y, size_z = dims
    cells = size_x * size_y * size_z
    tiles = n_flow * n_cross
    grains = geo_ref.shape[0]
    blocks = column_ref.shape[0]
    per_grain = blocks // grains
    lanes = off_ref.shape[-1]
    flow, cross, depth = (lax.axis_index("flow"), lax.axis_index("cross"), lax.axis_index("depth"))

    def group_at(slot):
        rf, rc = divmod(slot, n_cross)
        return (lax.rem(flow + rf, n_flow), lax.rem(cross + rc, n_cross), depth)

    def group_back(slot):
        rf, rc = divmod(slot, n_cross)
        return (
            lax.rem(flow + n_flow - rf, n_flow),
            lax.rem(cross + n_cross - rc, n_cross),
            depth,
        )

    def depth_at(rd):
        return (flow, cross, lax.rem(depth + rd, n_depth))

    slot_flow = {1: (n_flow - 1) * n_cross, -1: (1 % n_flow) * n_cross}
    slot_cross = {1: n_cross - 1, -1: 1 % n_cross}
    near_slots = sorted({slot_flow[1], slot_flow[-1], slot_cross[1], slot_cross[-1]} - {0})
    far_slots = [r for r in range(1, tiles) if r not in near_slots]
    near_slots = sorted(near_slots, key=lambda r: r // n_cross)
    order = near_slots + far_slots
    near_depth = sorted({1, n_depth - 1})
    depth_index = {1: near_depth.index(n_depth - 1), -1: near_depth.index(1)}

    barrier = pltpu.get_barrier_semaphore()
    for r in range(1, tiles):
        pl.semaphore_signal(barrier, inc=1, device_id=group_at(r), device_id_type=MESH)
    for rd in range(1, n_depth):
        pl.semaphore_signal(barrier, inc=1, device_id=depth_at(rd), device_id_type=MESH)
    pl.semaphore_wait(barrier, tiles - 1 + n_depth - 1)

    sent = []

    def ship(src, dst, send_sem, recv_sem, device):
        copy = pltpu.make_async_remote_copy(
            src_ref=src,
            dst_ref=dst,
            send_sem=send_sem,
            recv_sem=recv_sem,
            device_id=device,
            device_id_type=MESH,
        )
        copy.start()
        sent.append(copy)
        return copy

    off_copies = {}
    for r in order:
        off_copies[r] = ship(
            off_ref, off_group.at[r], off_send.at[r], off_recv.at[r], group_at(r)
        )
    off_depth_copies = []
    for i, rd in enumerate(near_depth):
        off_depth_copies.append(
            ship(
                off_ref,
                off_depth.at[i],
                off_send.at[tiles + i],
                off_recv.at[tiles + i],
                depth_at(rd),
            )
        )
    off_group[0] = off_ref[...]

    part = lax.rem(lax.broadcasted_iota(jnp.int32, (per_grain * COLS, lanes), 0), COLS)
    row = lax.broadcasted_iota(jnp.int32, (COLS, lanes), 0)
    block_lane = lax.broadcasted_iota(jnp.int32, (lanes, per_grain * COLS), 1) // COLS

    def turn(g, carry):
        rows = geo_ref[g]
        high = rounded(rows)
        low = rows - high
        low = jnp.concatenate([low[3:], low[:3]], axis=0)
        mix = jnp.where(part < 3, low, jnp.where(part < 6, high, 0.0))
        geo_turned[g] = jnp.transpose(mix)
        return carry

    def own_pass(slot, carry):
        done = []
        for cell in range(cells):
            own = [off_group[slot, c * cells + cell : c * cells + cell + 1, :] for c in range(3)]
            square = own[0] * own[0] + own[1] * own[1] + own[2] * own[2] - SHIFT
            base = jnp.where(row == 4, -square, 0.0)
            for c in range(3):
                base = jnp.where(row == c, 2.0 * own[c], base)
            high, middle, low = three_parts(base)
            high = jnp.where(row == 3, -1.0, high)
            features = jnp.concatenate([high, middle, low, high, middle, high], axis=0)
            done.append(jnp.transpose(features).astype(jnp.bfloat16))
        for cell in range(cells):
            own_features[slot * cells + cell] = done[cell]
        return carry

    lax.fori_loop(0, grains, turn, 0)
    for r in order:
        off_copies[r].wait_recv()
    lax.fori_loop(0, tiles, own_pass, 0)

    one_hot_row = (
        lax.broadcasted_iota(jnp.int32, (tiles * cells, blocks), 0) == row_ref[...]
    ).astype(jnp.float32)

    def marker_pass(g, carry):
        shift = shift_rows[g]
        turned = geo_turned[g]
        total = None
        for b in range(per_grain):
            place = slot_ref[g * per_grain + b] * cells + cell_ref[g * per_grain + b]
            point = jnp.where(row < 3, geo_ref[g, b * COLS : (b + 1) * COLS, :] + shift, 0.0)
            square = jnp.sum(point * point, axis=0, keepdims=True)
            point = jnp.where(row == 3, square, jnp.where(row == 4, 1.0, point))
            high, middle, low = three_parts(point)
            features = jnp.concatenate([high, high, high, middle, middle, low], axis=0)
            weight = jnp.exp2(
                jnp.dot(
                    own_features[place],
                    features.astype(jnp.bfloat16),
                    preferred_element_type=jnp.float32,
                )
            )
            upper = weight.astype(jnp.bfloat16)
            lower = (weight - upper.astype(jnp.float32)).astype(jnp.bfloat16)
            normals = jnp.where(block_lane == b, turned, 0.0).astype(jnp.bfloat16)
            term = jnp.dot(
                jnp.concatenate([upper, lower], axis=1),
                jnp.concatenate([normals, normals], axis=0),
                preferred_element_type=jnp.float32,
            )
            total = term if total is None else total + term
        total = jnp.transpose(total).reshape(per_grain, COLS, lanes)
        for c in range(3):
            normal_sums[c, pl.ds(pl.multiple_of(g * per_grain, 8), per_grain), :] = (
                total[:, c, :] + total[:, c + 3, :]
            )
        return carry

    lane = lax.rem(lax.broadcasted_iota(jnp.int32, (grains, lanes), 1), COLS)
    speed = start_ref[...]
    moved = jnp.zeros((grains, lanes), jnp.float32)
    velocity = [jnp.broadcast_to(speed[:, c : c + 1], (grains, lanes)) for c in range(3)]
    displace = [moved, moved, moved]

    def to_fluid(step):
        added = None
        for c in range(3):
            term = normal_sums[c].reshape(grains, per_grain, lanes) * velocity[c][:, None, :]
            added = term if added is None else added + term
        spread = jnp.dot(
            one_hot_row,
            added.reshape(blocks, lanes),
            precision=HIGHEST,
            preferred_element_type=jnp.float32,
        )
        give[step] = spread.reshape(tiles, cells, lanes)
        return [
            ship(
                give.at[step, r],
                take.at[step, r],
                take_send.at[step, r],
                take_recv.at[step, r],
                group_back(r),
            )
            for r in reversed(order)
        ]

    def collect(step, copies):
        total = give[step, 0]
        for copy in copies:
            copy.wait_recv()
        for r in range(1, tiles):
            total = total + take[step, r]
        return total

    merged = size_x == 1 and n_flow == 2
    sources = {("own", 0): 0}
    flow_keys = [("flow", 1)] if merged else [("flow", 1), ("flow", -1)]
    for key in flow_keys + [("cross", 1), ("cross", -1), ("depth", 1), ("depth", -1)]:
        sources[key] = len(sources)
    padded_rows = -(-len(sources) * cells // 128) * 128

    def columns_of(pick):
        rows = []
        for axis, side in sources:
            if axis == "own":
                rows.append(pick(0, None))
            elif axis == "flow":
                rows.append(pick(slot_flow[side], None))
            elif axis == "cross":
                rows.append(pick(slot_cross[side], None))
            else:
                rows.append(pick(None, depth_index[side]))
        spare = padded_rows - len(sources) * cells
        if spare:
            rows.append(jnp.zeros((spare, lanes), jnp.float32))
        return jnp.transpose(jnp.concatenate(rows, axis=0))

    def pairs(cell):
        x, rest = divmod(cell, size_y * size_z)
        y, z = divmod(rest, size_z)
        found = [(cell, (0, 0, 0))]
        place, extent, names = (x, y, z), (size_x, size_y, size_z), ("flow", "cross", "depth")
        for axis in range(3):
            for side in (1, -1):
                near = list(place)
                near[axis] += side
                key = ("own", 0)
                if not 0 <= near[axis] < extent[axis]:
                    near[axis] %= extent[axis]
                    key = (names[axis], side)
                    if axis == 0 and merged:
                        key = (names[axis], 1)
                index = (near[0] * size_y + near[1]) * size_z + near[2]
                step = [0, 0, 0]
                step[axis] = side
                found.append((sources[key] * cells + index, tuple(step)))
        return found

    groups = []
    for cell in range(cells):
        by_column = {}
        for column, step in pairs(cell):
            by_column.setdefault(column, []).append(step)
        groups.append(list(by_column.items()))

    shift_rows[...] = jnp.zeros(shift_rows.shape, jnp.float32)
    lax.fori_loop(0, grains, marker_pass, 0)
    copies = to_fluid(0)
    for copy in off_depth_copies:
        copy.wait_recv()

    turned = [
        columns_of(
            lambda slot, i, c=c: (
                off_group[slot, c * cells : (c + 1) * cells, :]
                if i is None
                else off_depth[i, c * cells : (c + 1) * cells, :]
            )
        )
        for c in range(3)
    ]
    sum_rows = []
    for cell in range(cells):
        own = [off_ref[c * cells + cell : c * cells + cell + 1, :] for c in range(3)]
        full = None
        for position, (column, steps) in enumerate(groups[cell]):
            total = None
            for step in steps:
                weight = weight_of(
                    [
                        turned[c][:, column : column + 1] - (own[c] - SCALE * step[c])
                        for c in range(3)
                    ]
                )
                total = weight if total is None else total + weight
            weights[cell, position] = total
            full = total if full is None else full + total
        sum_rows.append(jnp.sum(full, axis=0, keepdims=True))
    rowsum = jnp.concatenate(sum_rows, axis=0)
    diagonal = STIFFEN + rowsum - PER_PARTICLE
    inverse = 1.0 / diagonal

    def weighted(step, j):
        turned_field = columns_of(
            lambda slot, i: krylov[step, j, slot] if i is None else krylov_depth[step, j, i]
        )
        rows = []
        for cell in range(cells):
            total = None
            for low in range(0, lanes, 64):
                acc = None
                for position, (column, _) in enumerate(groups[cell]):
                    term = (
                        weights[cell, position, low : low + 64, :]
                        * turned_field[low : low + 64, column : column + 1]
                    )
                    acc = term if acc is None else acc + term
                acc = jnp.sum(acc.reshape(8, 8, lanes), axis=0)
                total = acc if total is None else total + acc
            rows.append(jnp.sum(total, axis=0, keepdims=True))
        return jnp.concatenate(rows, axis=0)

    pressure = jnp.zeros((cells, lanes), jnp.float32)
    spread_before = None
    residual = None
    pressure_all = None
    one_hot_column = (
        lax.broadcasted_iota(jnp.int32, (blocks, tiles * cells), 1) == column_ref[...]
    ).astype(jnp.float32)
    for step in range(STEPS):
        if step:
            shift = jnp.zeros(shift_rows.shape, jnp.float32)
            component = lax.broadcasted_iota(jnp.int32, shift_rows.shape, 1)
            for c in range(3):
                shift = jnp.where(component == c, SCALE * displace[c][:, None, :], shift)
            shift_rows[...] = shift
            lax.fori_loop(0, grains, marker_pass, 0)
            copies = to_fluid(step)
        spread = collect(step, copies)
        if step == 0:
            residual = source_ref[...] + spread
        else:
            residual = residual + (spread - spread_before)
        spread_before = spread
        fields = [residual * inverse]
        far = []
        for j in range(ITERS):
            krylov[step, j, 0] = fields[j]
            near = {}
            for r in near_slots:
                near[r] = ship(
                    krylov.at[step, j, 0],
                    krylov.at[step, j, r],
                    kry_send.at[step, j, r],
                    kry_recv.at[step, j, r],
                    group_at(r),
                )
            beside = [
                ship(
                    krylov.at[step, j, 0],
                    krylov_depth.at[step, j, i],
                    kry_send.at[step, j, tiles + i],
                    kry_recv.at[step, j, tiles + i],
                    depth_at(rd),
                )
                for i, rd in enumerate(near_depth)
            ]
            for r in far_slots:
                far.append(
                    ship(
                        krylov.at[step, j, 0],
                        krylov.at[step, j, r],
                        kry_send.at[step, j, r],
                        kry_recv.at[step, j, r],
                        group_at(r),
                    )
                )
            for copy in list(near.values()) + beside:
                copy.wait_recv()
            fields.append((weighted(step, j) - PER_PARTICLE * fields[j]) * inverse)
        moments = []
        for j in range(ITERS):
            scaled = diagonal * fields[j]
            moments.append(jnp.sum(scaled * fields[j], axis=0, keepdims=True))
            moments.append(jnp.sum(scaled * fields[j + 1], axis=0, keepdims=True))
        part_group[step, 0] = jnp.concatenate(moments, axis=0)
        waits = [
            ship(
                part_group.at[step, 0],
                part_group.at[step, r],
                part_send.at[step, r],
                part_recv.at[step, r],
                group_at(r),
            )
            for r in order
        ]
        for copy in waits:
            copy.wait_recv()
        total = part_group[step, 0]
        for r in range(1, tiles):
            total = total + part_group[step, r]
        part_depth[step, 0] = total
        waits = [
            ship(
                part_depth.at[step, 0],
                part_depth.at[step, rd],
                part_send.at[step, tiles + rd],
                part_recv.at[step, tiles + rd],
                depth_at(rd),
            )
            for rd in range(1, n_depth)
        ]
        for copy in waits:
            copy.wait_recv()
        for rd in range(1, n_depth):
            total = total + part_depth[step, rd]
        total = jnp.broadcast_to(jnp.sum(total, axis=1, keepdims=True), total.shape)
        scalars = [total[q : q + 1, :] for q in range(2 * ITERS)]
        gram = [
            [scalars[i + j] - scalars[i + j + 1] for j in range(ITERS)] for i in range(ITERS)
        ]
        factors = solve_small(gram, scalars[:ITERS])
        for j in range(ITERS):
            pressure = pressure + factors[j] * fields[j]
            residual = residual - factors[j] * (diagonal * (fields[j] - fields[j + 1]))
        for copy in far:
            copy.wait_recv()
        for j in range(ITERS):
            term = factors[j] * krylov[step, j].reshape(tiles * cells, lanes)
            pressure_all = term if pressure_all is None else pressure_all + term
        felt = jnp.dot(
            one_hot_column,
            pressure_all,
            precision=HIGHEST,
            preferred_element_type=jnp.float32,
        )
        for c in range(3):
            force = (normal_sums[c] * felt).reshape(grains, per_grain, lanes)
            force = jnp.sum(jnp.sum(force, axis=1), axis=1, keepdims=True)
            velocity[c] = velocity[c] + STEP_TIME * force / mass_ref[...]
            displace[c] = displace[c] + STEP_TIME * velocity[c]
    press_out[...] = pressure
    speed = jnp.zeros((grains, lanes), jnp.float32)
    for c in range(3):
        speed = jnp.where(lane == c, velocity[c], speed)
    speed_out[...] = speed
    for copy in sent:
        copy.wait_send()


def per_device(
    sizes,
    fluid_offsets,
    source,
    marker_offsets,
    marker_normals,
    dest_tile,
    cell_index,
    grain_velocity,
    grain_mass,
):
    n_flow, n_cross, n_depth = sizes
    tiles = n_flow * n_cross
    dims = source.shape[:3]
    cells = dims[0] * dims[1] * dims[2]
    lanes = source.shape[3]
    grains, per_grain = cell_index.shape
    blocks = grains * per_grain
    tile = dest_tile.reshape(blocks)
    slot_flow = (lax.axis_index("flow") - tile // n_cross) % n_flow
    slot_cross = (lax.axis_index("cross") - tile % n_cross) % n_cross
    slot = (slot_flow * n_cross + slot_cross).astype(jnp.int32)
    cell = cell_index.reshape(blocks)
    place = slot * cells + cell
    offsets = (fluid_offsets * SCALE).reshape(3 * cells, lanes)
    geometry = jnp.concatenate(
        [
            marker_offsets * SCALE,
            marker_normals,
            jnp.zeros((grains, per_grain, COLS - 6, lanes), jnp.float32),
        ],
        axis=2,
    ).reshape(grains, per_grain * COLS, lanes)
    start = jnp.pad(grain_velocity, ((0, 0), (0, lanes - 3)))
    mass = jnp.broadcast_to(grain_mass[:, None], (grains, lanes))
    near_count = len({1, n_depth - 1})
    vmem, dma = pltpu.VMEM, pltpu.SemaphoreType.DMA
    f32 = jnp.float32
    in_vmem = pl.BlockSpec(memory_space=pltpu.VMEM)
    in_smem = pl.BlockSpec(memory_space=pltpu.SMEM)
    pressure, speed = pl.pallas_call(
        functools.partial(kernel, sizes, dims),
        out_shape=(
            jax.ShapeDtypeStruct((cells, lanes), f32),
            jax.ShapeDtypeStruct((grains, lanes), f32),
        ),
        in_specs=[in_smem] * 2 + [in_vmem] * 7,
        out_specs=(in_vmem, in_vmem),
        scratch_shapes=[
            vmem((tiles, 3 * cells, lanes), f32),
            vmem((near_count, 3 * cells, lanes), f32),
            vmem((cells, 7, lanes, lanes), f32),
            vmem((grains, lanes, per_grain * COLS), f32),
            vmem((tiles * cells, lanes, 6 * COLS), jnp.bfloat16),
            vmem((grains, COLS, lanes), f32),
            vmem((3, blocks, lanes), f32),
            vmem((STEPS, tiles, cells, lanes), f32),
            vmem((STEPS, tiles, cells, lanes), f32),
            vmem((STEPS, ITERS, tiles, cells, lanes), f32),
            vmem((STEPS, ITERS, near_count, cells, lanes), f32),
            vmem((STEPS, tiles, 2 * ITERS, lanes), f32),
            vmem((STEPS, n_depth, 2 * ITERS, lanes), f32),
            dma((tiles + near_count,)),
            dma((tiles + near_count,)),
            dma((STEPS, tiles)),
            dma((STEPS, tiles)),
            dma((STEPS, ITERS, tiles + near_count)),
            dma((STEPS, ITERS, tiles + near_count)),
            dma((STEPS, tiles + n_depth)),
            dma((STEPS, tiles + n_depth)),
        ],
        compiler_params=pltpu.CompilerParams(
            collective_id=0, has_side_effects=True, vmem_limit_bytes=60 * 1024 * 1024
        ),
        name="coupled",
    )(
        slot,
        cell,
        offsets,
        source.reshape(cells, lanes),
        geometry,
        start,
        mass,
        place[:, None],
        place[None, :],
    )
    return (pressure.reshape(source.shape), speed[:, :3])


def solution(mesh):
    sizes = tuple(mesh.shape[name] for name in ("flow", "cross", "depth"))
    return jax.shard_map(
        functools.partial(per_device, sizes),
        mesh=mesh,
        in_specs=(
            P(None, "flow", "cross", "depth", None),
            P("flow", "cross", "depth", None),
            P(("flow", "cross", "depth"), None, None, None),
            P(("flow", "cross", "depth"), None, None, None),
            P(("flow", "cross", "depth"), None, None),
            P(("flow", "cross", "depth"), None),
            P(("flow", "cross", "depth"), None),
            P(("flow", "cross", "depth")),
        ),
        out_specs=(P("flow", "cross", "depth", None), P(("flow", "cross", "depth"), None)),
        check_vma=False,
    )
```

profile of v0, /device:TPU:0, one launch (start us, length us, event | category | flops | bytes accessed | tf_op | source)
XLA Modules:
  0.0 145.4 jit_solution(13881164702283440082)
XLA Ops:
  0.6 0.5 broadcast.373
  1.1 0.0 copy-start.3
  1.1 1.4 reduce.7
  2.5 0.1 reshape.403
  2.6 0.6 fusion.10.slot_ref
  3.2 0.1 copy-done.1
  3.3 0.7 reshape.404.cell_ref
  4.0 0.0 copy-done.3
  4.0 0.6 broadcast_multiply_fusion.1
  4.6 1.1 broadcast_multiply_fusion
  5.7 0.1 pad.7.clone
  5.8 0.0 copy-done
  5.8 0.2 maximum_maximum_fusion
  5.9 0.0 copy-start.5
  5.9 1.3 copy.22
  7.3 0.0 copy-done.5
  7.3 0.1 copy.14
  7.3 0.6 pad.4.start_ref
  8.0 0.1 copy-done.6
  8.0 0.7 broadcast_in_dim.5.mass_ref
  8.7 0.1 reshape.414
  8.8 0.6 copy-done.2
  9.4 0.1 reshape.413
  9.5 0.9 fusion.5.column_ref
  10.4 0.1 reshape.411
  10.4 0.1 reshape.410
  10.5 0.6 multiply_add_fusion.row_ref
  11.1 132.3 %coupled.1 = (f32[16,128]{1,0:T(8,128)}, f32[16,128]{1,0:T(8,128)}) custom-call(s32[256]{0:T(256)} %fusion.10.slot_ref, s32[256]{0:T(256)} %reshape.404.cell_ref, f32[48,128]{1,0:T(8,128)} %bitcast.10, f32[16,128]{1,0:T(8,128)} %bitcast.13, f32[16,128,128]{2,1,0:T(8,128)} %bitcast.9, f32[16,128]{1,0:T(8,128)} %pad.4.start_ref, ...), custom_call_target="tpu_custom_call" | custom-call | tf_op jit(solution)/shard_map/coupled/pallas_call | solution.py:555
  143.4 0.0 copy-start.4
  143.4 1.4 copy.20
  144.8 0.0 copy-done.4
  144.8 0.6 copy.24
  (5 shorter events, 0.0 us)
Async XLA Ops:
  1.1 2.8 %copy-start.3 = (f32[3,1,4,4,128]{4,3,2,1,0:T(4,128)S(1)}, f32[3,1,4,4,128]{4,3,2,1,0:T(4,128)}, u32[]{:S(2)}) copy-start(f32[3,1,4,4,128]{4,3,2,1,0:T(4,128)} %param.8) | copy-start | bytes 73732
  2.6 0.7 copy-start.1
  4.6 1.2 copy-start
  5.9 1.3 copy-start.5
  7.3 0.7 copy-start.6
  8.7 0.7 copy-start.2
  143.4 1.4 copy-start.4
where the time goes:
time: 146 us; the launch traced here: 145 us
  Pallas kernels  132 us (90%)
  local copies, waits for them, and re-layouts  7.08 us (5%)
  other arithmetic  5.31 us (4%)
    pallas_call x1, Pallas kernels, per_device(): pl.pallas_call(functools.partial(kernel, sizes, dims), out_shape=(jax.Sha...  132 us
    unnamed x18, local copies, waits for them, and re-layouts  3.33 us

commit v1 on v0

--- a/solution.py
+++ b/solution.py
@@ -16,8 +16,9 @@
 SCALE = math.sqrt(math.log2(math.e))
 SHIFT = math.log2(PER_PARTICLE)
 MESH = pl.DeviceIdType.MESH
-HIGHEST = lax.Precision.HIGHEST
-COLS = 8
+ROWS = 8
+GROUP = 4
+MIDDLE = 0.5
 
 
 def weight_of(gaps):
@@ -29,12 +30,6 @@
 
 def rounded(value):
     return value.astype(jnp.bfloat16).astype(jnp.float32)
-
-
-def three_parts(value):
-    high = rounded(value)
-    middle = rounded(value - high)
-    return high, middle, (value - high) - middle
 
 
 def solve_small(gram, right):
@@ -57,27 +52,44 @@
     return out
 
 
+def two_parts(value):
+    high = rounded(value)
+    return high, value - high
+
+
 def kernel(
     sizes,
     dims,
-    slot_ref,
-    cell_ref,
     off_ref,
     source_ref,
-    geo_ref,
+    points_ref,
+    normals_ref,
+    tile_ref,
+    cell_ref,
     start_ref,
     mass_ref,
-    column_ref,
-    row_ref,
     press_out,
     speed_out,
     off_group,
     off_depth,
     weights,
-    geo_turned,
-    own_features,
-    shift_rows,
+    own_rows,
+    own_columns,
+    point_rows,
+    point_parts,
+    normal_rows,
+    normal_parts,
+    near,
     normal_sums,
+    added,
+    felt_rows,
+    speed_rows,
+    mass_rows,
+    moved_rows,
+    own_shift,
+    point_shift,
+    place_rows,
+    place_ref,
     give,
     take,
     krylov,
@@ -92,15 +104,14 @@
     kry_recv,
     part_send,
     part_recv,
+    place_sem,
 ):
     n_flow, n_cross, n_depth = sizes
     size_x, size_y, size_z = dims
     cells = size_x * size_y * size_z
     tiles = n_flow * n_cross
-    grains = geo_ref.shape[0]
-    blocks = column_ref.shape[0]
-    per_grain = blocks // grains
-    lanes = off_ref.shape[-1]
+    grains, _, per_grain, lanes = points_ref.shape
+    blocks = grains * per_grain
     flow, cross, depth = (lax.axis_index("flow"), lax.axis_index("cross"), lax.axis_index("depth"))
 
     def group_at(slot):
@@ -132,6 +143,62 @@
         pl.semaphore_signal(barrier, inc=1, device_id=group_at(r), device_id_type=MESH)
     for rd in range(1, n_depth):
         pl.semaphore_signal(barrier, inc=1, device_id=depth_at(rd), device_id_type=MESH)
+
+    row = lax.broadcasted_iota(jnp.int32, (ROWS, lanes), 0)
+
+    tile = tile_ref[:, 0, :]
+    slot_flow_of = lax.rem(flow + n_flow - lax.div(tile, n_cross), n_flow)
+    slot_cross_of = lax.rem(cross + n_cross - lax.rem(tile, n_cross), n_cross)
+    slot_of = slot_flow_of * n_cross + slot_cross_of
+    place_rows[...] = jnp.zeros(place_rows.shape, jnp.int32)
+    place_rows[:, :per_grain] = slot_of * cells + cell_ref[...]
+    place_copy = pltpu.make_async_copy(place_rows, place_ref, place_sem)
+    place_copy.start()
+
+    spot = lax.broadcasted_iota(jnp.int32, (per_grain, blocks), 1)
+    pick = (
+        lax.rem(spot, per_grain) == lax.broadcasted_iota(jnp.int32, (per_grain, blocks), 0)
+    ).astype(jnp.bfloat16)
+    held = (
+        lax.div(lax.broadcasted_iota(jnp.int32, (grains, blocks), 1), per_grain)
+        == lax.broadcasted_iota(jnp.int32, (grains, blocks), 0)
+    )
+
+    def in_a_row(value):
+        spread = jnp.dot(
+            value.astype(jnp.float32).astype(jnp.bfloat16),
+            pick,
+            preferred_element_type=jnp.float32,
+        )
+        return jnp.sum(jnp.where(held, spread, 0.0), axis=0, keepdims=True)
+
+    place_row = in_a_row(slot_of) * cells + in_a_row(cell_ref[...])
+    one_hot = jnp.where(
+        lax.broadcasted_iota(jnp.int32, (tiles * cells, blocks), 0).astype(jnp.float32)
+        == place_row,
+        1.0,
+        0.0,
+    ).astype(jnp.bfloat16)
+
+    def prepare(g, carry):
+        for b in range(per_grain):
+            point = jnp.where(row > 3, 1.0, 0.0)
+            normal = jnp.zeros((ROWS, lanes), jnp.float32)
+            for c in range(3):
+                point = jnp.where(
+                    row == c, SCALE * (points_ref[g, c, b : b + 1, :] - MIDDLE), point
+                )
+                normal = jnp.where(row == c, normals_ref[g, c, b : b + 1, :], normal)
+            square = jnp.sum(jnp.where(row < 3, point * point, 0.0), axis=0, keepdims=True)
+            point = jnp.where(row == 3, square, point)
+            point_rows[g, b] = point
+            point_parts[g, b] = jnp.concatenate(two_parts(point), axis=0).astype(jnp.bfloat16)
+            normal_rows[g, b] = normal
+            normal_parts[g, b] = jnp.concatenate(two_parts(normal), axis=0).astype(jnp.bfloat16)
+        return carry
+
+    lax.fori_loop(0, grains, prepare, 0)
+    place_copy.wait()
     pl.semaphore_wait(barrier, tiles - 1 + n_depth - 1)
 
     sent = []
@@ -167,95 +234,100 @@
         )
     off_group[0] = off_ref[...]
 
-    part = lax.rem(lax.broadcasted_iota(jnp.int32, (per_grain * COLS, lanes), 0), COLS)
-    row = lax.broadcasted_iota(jnp.int32, (COLS, lanes), 0)
-    block_lane = lax.broadcasted_iota(jnp.int32, (lanes, per_grain * COLS), 1) // COLS
-
-    def turn(g, carry):
-        rows = geo_ref[g]
-        high = rounded(rows)
-        low = rows - high
-        low = jnp.concatenate([low[3:], low[:3]], axis=0)
-        mix = jnp.where(part < 3, low, jnp.where(part < 6, high, 0.0))
-        geo_turned[g] = jnp.transpose(mix)
+    def own_pass(slot, carry):
+        for low in range(0, cells, GROUP):
+            stacked = []
+            for cell in range(low, low + GROUP):
+                base = jnp.where(row == 3, -1.0, jnp.where(row == 5, SHIFT, 0.0))
+                square = None
+                for c in range(3):
+                    spot = c * cells + cell
+                    own = SCALE * (off_group[slot, spot : spot + 1, :] - MIDDLE)
+                    base = jnp.where(row == c, 2.0 * own, base)
+                    square = own * own if square is None else square + own * own
+                base = jnp.where(row == 4, -square, base)
+                own_rows[slot * cells + cell] = base
+                high, rest = two_parts(base)
+                stacked += [high, high, rest, rest]
+            own_columns[slot * (cells // GROUP) + low // GROUP] = jnp.transpose(
+                jnp.concatenate(stacked, axis=0)
+            ).astype(jnp.bfloat16)
         return carry
 
-    def own_pass(slot, carry):
-        done = []
-        for cell in range(cells):
-            own = [off_group[slot, c * cells + cell : c * cells + cell + 1, :] for c in range(3)]
-            square = own[0] * own[0] + own[1] * own[1] + own[2] * own[2] - SHIFT
-            base = jnp.where(row == 4, -square, 0.0)
-            for c in range(3):
-                base = jnp.where(row == c, 2.0 * own[c], base)
-            high, middle, low = three_parts(base)
-            high = jnp.where(row == 3, -1.0, high)
-            features = jnp.concatenate([high, middle, low, high, middle, high], axis=0)
-            done.append(jnp.transpose(features).astype(jnp.bfloat16))
-        for cell in range(cells):
-            own_features[slot * cells + cell] = done[cell]
-        return carry
-
-    lax.fori_loop(0, grains, turn, 0)
     for r in order:
         off_copies[r].wait_recv()
     lax.fori_loop(0, tiles, own_pass, 0)
 
-    one_hot_row = (
-        lax.broadcasted_iota(jnp.int32, (tiles * cells, blocks), 0) == row_ref[...]
-    ).astype(jnp.float32)
-
-    def marker_pass(g, carry):
-        shift = shift_rows[g]
-        turned = geo_turned[g]
-        total = None
+    def near_pass(g, carry):
         for b in range(per_grain):
-            place = slot_ref[g * per_grain + b] * cells + cell_ref[g * per_grain + b]
-            point = jnp.where(row < 3, geo_ref[g, b * COLS : (b + 1) * COLS, :] + shift, 0.0)
-            square = jnp.sum(point * point, axis=0, keepdims=True)
-            point = jnp.where(row == 3, square, jnp.where(row == 4, 1.0, point))
-            high, middle, low = three_parts(point)
-            features = jnp.concatenate([high, high, high, middle, middle, low], axis=0)
+            place = place_ref[g, b]
+            member = lax.rem(place, GROUP)
+            parts = point_parts[g, b]
+            stacked = []
+            for k in range(GROUP):
+                picked = jnp.where(member == k, parts, jnp.zeros_like(parts))
+                stacked += [picked, picked]
             weight = jnp.exp2(
                 jnp.dot(
-                    own_features[place],
-                    features.astype(jnp.bfloat16),
+                    own_columns[lax.div(place, GROUP)],
+                    jnp.concatenate(stacked, axis=0),
                     preferred_element_type=jnp.float32,
                 )
             )
             upper = weight.astype(jnp.bfloat16)
-            lower = (weight - upper.astype(jnp.float32)).astype(jnp.bfloat16)
-            normals = jnp.where(block_lane == b, turned, 0.0).astype(jnp.bfloat16)
-            term = jnp.dot(
-                jnp.concatenate([upper, lower], axis=1),
-                jnp.concatenate([normals, normals], axis=0),
-                preferred_element_type=jnp.float32,
-            )
-            total = term if total is None else total + term
-        total = jnp.transpose(total).reshape(per_grain, COLS, lanes)
-        for c in range(3):
-            normal_sums[c, pl.ds(pl.multiple_of(g * per_grain, 8), per_grain), :] = (
-                total[:, c, :] + total[:, c + 3, :]
+            near[g * per_grain + b, :, :lanes] = upper
+            near[g * per_grain + b, :, lanes:] = (weight - upper.astype(jnp.float32)).astype(
+                jnp.bfloat16
             )
         return carry
 
-    lane = lax.rem(lax.broadcasted_iota(jnp.int32, (grains, lanes), 1), COLS)
-    speed = start_ref[...]
-    moved = jnp.zeros((grains, lanes), jnp.float32)
-    velocity = [jnp.broadcast_to(speed[:, c : c + 1], (grains, lanes)) for c in range(3)]
-    displace = [moved, moved, moved]
+    lax.fori_loop(0, grains, near_pass, 0)
+
+    def weigh(step, velocity, own_shift, point_shift):
+        def body(g, carry):
+            rows = []
+            half = lax.broadcasted_iota(jnp.int32, (per_grain, lanes), 0)
+            rates = jnp.zeros((per_grain, lanes), jnp.float32)
+            for b in range(per_grain):
+                if step:
+                    factor = jnp.exp2(
+                        jnp.sum(point_rows[g, b] * point_shift[g], axis=0, keepdims=True)
+                    )
+                    parts = jnp.concatenate(
+                        two_parts(normal_rows[g, b] * factor), axis=0
+                    ).astype(jnp.bfloat16)
+                else:
+                    parts = normal_parts[g, b]
+                total = lax.dot_general(
+                    jnp.concatenate([parts, parts], axis=1),
+                    near[g * per_grain + b],
+                    (((1,), (1,)), ((), ())),
+                    preferred_element_type=jnp.float32,
+                )
+                total = total[:ROWS] + total[ROWS:]
+                if step:
+                    factor = jnp.exp2(
+                        jnp.sum(
+                            own_rows[place_ref[g, b]] * own_shift[g], axis=0, keepdims=True
+                        )
+                    )
+                    total = total * factor
+                normal_sums[g, b] = total
+                rate = jnp.sum(total * velocity[g], axis=0, keepdims=True)
+                rates = jnp.where(half == b, rate, rates)
+            added[pl.ds(pl.multiple_of(g * per_grain, ROWS), per_grain), :] = rates
+            return carry
+
+        lax.fori_loop(0, grains, body, 0)
 
     def to_fluid(step):
-        added = None
-        for c in range(3):
-            term = normal_sums[c].reshape(grains, per_grain, lanes) * velocity[c][:, None, :]
-            added = term if added is None else added + term
+        high, rest = two_parts(added[...])
         spread = jnp.dot(
-            one_hot_row,
-            added.reshape(blocks, lanes),
-            precision=HIGHEST,
+            one_hot,
+            jnp.concatenate([high, rest], axis=1).astype(jnp.bfloat16),
             preferred_element_type=jnp.float32,
         )
+        spread = spread[:, :lanes] + spread[:, lanes:]
         give[step] = spread.reshape(tiles, cells, lanes)
         return [
             ship(
@@ -327,14 +399,23 @@
             by_column.setdefault(column, []).append(step)
         groups.append(list(by_column.items()))
 
-    shift_rows[...] = jnp.zeros(shift_rows.shape, jnp.float32)
-    lax.fori_loop(0, grains, marker_pass, 0)
+    start = jnp.zeros((ROWS, grains), jnp.float32)
+    grain_row = lax.broadcasted_iota(jnp.int32, (ROWS, grains), 0)
+    for c in range(3):
+        start = jnp.where(grain_row == c, start_ref[c : c + 1, :], start)
+    for g in range(grains):
+        speed_rows[g] = jnp.broadcast_to(start[:, g : g + 1], (ROWS, lanes))
+        mass_rows[g] = jnp.broadcast_to(mass_ref[:, g : g + 1], (ROWS, lanes))
+        moved_rows[g] = jnp.zeros((ROWS, lanes), jnp.float32)
+
+    weigh(0, speed_rows, None, None)
     copies = to_fluid(0)
     for copy in off_depth_copies:
         copy.wait_recv()
 
     turned = [
-        columns_of(
+        SCALE
+        * columns_of(
             lambda slot, i, c=c: (
                 off_group[slot, c * cells : (c + 1) * cells, :]
                 if i is None
@@ -345,7 +426,9 @@
     ]
     sum_rows = []
     for cell in range(cells):
-        own = [off_ref[c * cells + cell : c * cells + cell + 1, :] for c in range(3)]
+        own = [
+            SCALE * off_ref[c * cells + cell : c * cells + cell + 1, :] for c in range(3)
+        ]
         full = None
         for position, (column, steps) in enumerate(groups[cell]):
             total = None
@@ -388,17 +471,14 @@
     spread_before = None
     residual = None
     pressure_all = None
-    one_hot_column = (
-        lax.broadcasted_iota(jnp.int32, (blocks, tiles * cells), 1) == column_ref[...]
-    ).astype(jnp.float32)
     for step in range(STEPS):
         if step:
-            shift = jnp.zeros(shift_rows.shape, jnp.float32)
-            component = lax.broadcasted_iota(jnp.int32, shift_rows.shape, 1)
-            for c in range(3):
-                shift = jnp.where(component == c, SCALE * displace[c][:, None, :], shift)
-            shift_rows[...] = shift
-            lax.fori_loop(0, grains, marker_pass, 0)
+            for g in range(grains):
+                shift = SCALE * moved_rows[g]
+                square = 0.5 * jnp.sum(shift * shift, axis=0, keepdims=True)
+                own_shift[g] = jnp.where(row == 3, square, shift)
+                point_shift[g] = jnp.where(row == 4, -square, -2.0 * shift)
+            weigh(step, speed_rows, own_shift, point_shift)
             copies = to_fluid(step)
         spread = collect(step, copies)
         if step == 0:
@@ -410,9 +490,9 @@
         far = []
         for j in range(ITERS):
             krylov[step, j, 0] = fields[j]
-            near = {}
+            close = {}
             for r in near_slots:
-                near[r] = ship(
+                close[r] = ship(
                     krylov.at[step, j, 0],
                     krylov.at[step, j, r],
                     kry_send.at[step, j, r],
@@ -439,7 +519,7 @@
                         group_at(r),
                     )
                 )
-            for copy in list(near.values()) + beside:
+            for copy in list(close.values()) + beside:
                 copy.wait_recv()
             fields.append((weighted(step, j) - PER_PARTICLE * fields[j]) * inverse)
         moments = []
@@ -492,22 +572,29 @@
         for j in range(ITERS):
             term = factors[j] * krylov[step, j].reshape(tiles * cells, lanes)
             pressure_all = term if pressure_all is None else pressure_all + term
-        felt = jnp.dot(
-            one_hot_column,
-            pressure_all,
-            precision=HIGHEST,
-            preferred_element_type=jnp.float32,
-        )
-        for c in range(3):
-            force = (normal_sums[c] * felt).reshape(grains, per_grain, lanes)
-            force = jnp.sum(jnp.sum(force, axis=1), axis=1, keepdims=True)
-            velocity[c] = velocity[c] + STEP_TIME * force / mass_ref[...]
-            displace[c] = displace[c] + STEP_TIME * velocity[c]
+        felt_rows[...] = pressure_all
+
+        def push(g, carry):
+            total = None
+            for b in range(per_grain):
+                felt = felt_rows[pl.ds(place_ref[g, b], 1), :]
+                term = normal_sums[g, b] * felt
+                total = term if total is None else total + term
+            force = jnp.broadcast_to(
+                jnp.sum(total, axis=1, keepdims=True), (ROWS, lanes)
+            )
+            speed = speed_rows[g] + STEP_TIME * force / mass_rows[g]
+            speed_rows[g] = speed
+            moved_rows[g] = moved_rows[g] + STEP_TIME * speed
+            return carry
+
+        lax.fori_loop(0, grains, push, 0)
     press_out[...] = pressure
-    speed = jnp.zeros((grains, lanes), jnp.float32)
-    for c in range(3):
-        speed = jnp.where(lane == c, velocity[c], speed)
-    speed_out[...] = speed
+    lane = lax.broadcasted_iota(jnp.int32, (ROWS, lanes), 1)
+    speed = jnp.zeros((ROWS, lanes), jnp.float32)
+    for g in range(grains):
+        speed = jnp.where(lane == g, speed_rows[g], speed)
+    speed_out[...] = speed[:3, :grains]
     for copy in sent:
         copy.wait_send()
 
@@ -530,44 +617,39 @@
     lanes = source.shape[3]
     grains, per_grain = cell_index.shape
     blocks = grains * per_grain
-    tile = dest_tile.reshape(blocks)
-    slot_flow = (lax.axis_index("flow") - tile // n_cross) % n_flow
-    slot_cross = (lax.axis_index("cross") - tile % n_cross) % n_cross
-    slot = (slot_flow * n_cross + slot_cross).astype(jnp.int32)
-    cell = cell_index.reshape(blocks)
-    place = slot * cells + cell
-    offsets = (fluid_offsets * SCALE).reshape(3 * cells, lanes)
-    geometry = jnp.concatenate(
-        [
-            marker_offsets * SCALE,
-            marker_normals,
-            jnp.zeros((grains, per_grain, COLS - 6, lanes), jnp.float32),
-        ],
-        axis=2,
-    ).reshape(grains, per_grain * COLS, lanes)
-    start = jnp.pad(grain_velocity, ((0, 0), (0, lanes - 3)))
-    mass = jnp.broadcast_to(grain_mass[:, None], (grains, lanes))
     near_count = len({1, n_depth - 1})
     vmem, dma = pltpu.VMEM, pltpu.SemaphoreType.DMA
     f32 = jnp.float32
     in_vmem = pl.BlockSpec(memory_space=pltpu.VMEM)
-    in_smem = pl.BlockSpec(memory_space=pltpu.SMEM)
     pressure, speed = pl.pallas_call(
         functools.partial(kernel, sizes, dims),
         out_shape=(
             jax.ShapeDtypeStruct((cells, lanes), f32),
-            jax.ShapeDtypeStruct((grains, lanes), f32),
+            jax.ShapeDtypeStruct((3, grains), f32),
         ),
-        in_specs=[in_smem] * 2 + [in_vmem] * 7,
+        in_specs=[in_vmem] * 8,
         out_specs=(in_vmem, in_vmem),
         scratch_shapes=[
             vmem((tiles, 3 * cells, lanes), f32),
             vmem((near_count, 3 * cells, lanes), f32),
             vmem((cells, 7, lanes, lanes), f32),
-            vmem((grains, lanes, per_grain * COLS), f32),
-            vmem((tiles * cells, lanes, 6 * COLS), jnp.bfloat16),
-            vmem((grains, COLS, lanes), f32),
-            vmem((3, blocks, lanes), f32),
+            vmem((tiles * cells, ROWS, lanes), f32),
+            vmem((tiles * cells // GROUP, lanes, 4 * ROWS * GROUP), jnp.bfloat16),
+            vmem((grains, per_grain, ROWS, lanes), f32),
+            vmem((grains, per_grain, 2 * ROWS, lanes), jnp.bfloat16),
+            vmem((grains, per_grain, ROWS, lanes), f32),
+            vmem((grains, per_grain, 2 * ROWS, lanes), jnp.bfloat16),
+            vmem((blocks, lanes, 2 * lanes), jnp.bfloat16),
+            vmem((grains, per_grain, ROWS, lanes), f32),
+            vmem((blocks, lanes), f32),
+            vmem((tiles * cells, lanes), f32),
+            vmem((grains, ROWS, lanes), f32),
+            vmem((grains, ROWS, lanes), f32),
+            vmem((grains, ROWS, lanes), f32),
+            vmem((grains, ROWS, lanes), f32),
+            vmem((grains, ROWS, lanes), f32),
+            vmem((grains, lanes), jnp.int32),
+            pltpu.SMEM((grains, lanes), jnp.int32),
             vmem((STEPS, tiles, cells, lanes), f32),
             vmem((STEPS, tiles, cells, lanes), f32),
             vmem((STEPS, ITERS, tiles, cells, lanes), f32),
@@ -582,23 +664,23 @@
             dma((STEPS, ITERS, tiles + near_count)),
             dma((STEPS, tiles + n_depth)),
             dma((STEPS, tiles + n_depth)),
+            dma,
         ],
         compiler_params=pltpu.CompilerParams(
             collective_id=0, has_side_effects=True, vmem_limit_bytes=60 * 1024 * 1024
         ),
         name="coupled",
     )(
-        slot,
-        cell,
-        offsets,
+        fluid_offsets.reshape(3 * cells, lanes),
         source.reshape(cells, lanes),
-        geometry,
-        start,
-        mass,
-        place[:, None],
-        place[None, :],
+        jnp.transpose(marker_offsets, (0, 2, 1, 3)),
+        jnp.transpose(marker_normals, (0, 2, 1, 3)),
+        jnp.transpose(dest_tile, (0, 2, 1)),
+        cell_index,
+        jnp.transpose(grain_velocity),
+        grain_mass[None, :],
     )
-    return (pressure.reshape(source.shape), speed[:, :3])
+    return (pressure.reshape(source.shape), jnp.transpose(speed))
 
 
 def solution(mesh):

time: 146 us -> 105 us (0.72)
  Pallas kernels: 132 us -> 102 us
  other arithmetic: 5.31 us -> 0 us
  local copies, waits for them, and re-layouts: 7.08 us -> 1.88 us
    pallas_call x1, Pallas kernels: 132 us -> 102 us  [per_device(): pl.pallas_call(functools.partial(kernel, sizes, dims), out_shape=(jax.Sha...]
    add x3 -> x0, other arithmetic: 2.07 us -> none  [the longest x2 1.49 us: per_device(): place = slot * cells + cell]
    mul x2 -> x0, other arithmetic: 1.7 us -> none  [the longest x1 1.08 us: per_device(): marker_offsets * SCALE]
    unnamed x18 -> x4, local copies, waits for them, and re-layouts: 3.33 us -> 1.88 us
where the time goes in v1:
time: 105 us
  Pallas kernels  102 us (97%)
  local copies, waits for them, and re-layouts  1.88 us (2%)
    pallas_call x1, Pallas kernels, per_device(): pl.pallas_call(functools.partial(kernel, sizes, dims), out_shape=(jax.Sha...  102 us

profile of v1, /device:TPU:0, one launch (start us, length us, event | category | flops | bytes accessed | tf_op | source)
XLA Modules:
  0.0 104.7 jit_solution(4582728654368919877)
XLA Ops:
  0.6 102.2 %coupled.1 = (f32[16,128]{1,0:T(8,128)}, f32[3,16]{1,0:T(4,128)}) custom-call(f32[48,128]{1,0:T(8,128)} %bitcast.11, f32[16,128]{1,0:T(8,128)} %bitcast.12, f32[16,3,16,128]{3,2,1,0:T(8,128)} %bitcast.9, f32[16,3,16,128]{3,2,1,0:T(8,128)} %bitcast.10, s32[16,1,16]{2,1,0:T(1,128)} %bitcast.13, s32[16,16]{1,0:T(8,128)} %cell_ref.1, f32[3,16]{1,0:T(4,128)} %bitcast.15, ...), custom_call_target="tpu_custom_call" | custom-call | tf_op jit(solution)/shard_map/coupled/pallas_call | solution.py:624
  102.9 0.0 copy-start
  102.9 1.3 %copy.12 = f32[1,4,4,128]{3,2,1,0:T(4,128)} copy(f32[1,4,4,128]{3,2,1,0:T(4,128)} %bitcast.14) | data formatting | bytes 16384
  104.2 0.0 copy-done
  104.2 0.6 copy.13
Async XLA Ops:
  102.9 1.3 %copy-start = (f32[3,16]{1,0:T(4,128)S(1)}, f32[3,16]{1,0:T(4,128)}, u32[]{:S(2)}) copy-start(f32[3,16]{1,0:T(4,128)} %get-tuple-element.5) | copy-start | bytes 580

commit v2 on v1

--- a/solution.py
+++ b/solution.py
@@ -94,8 +94,7 @@
     take,
     krylov,
     krylov_depth,
-    part_group,
-    part_depth,
+    part,
     off_send,
     off_recv,
     take_send,
@@ -139,10 +138,14 @@
     depth_index = {1: near_depth.index(n_depth - 1), -1: near_depth.index(1)}
 
     barrier = pltpu.get_barrier_semaphore()
-    for r in range(1, tiles):
-        pl.semaphore_signal(barrier, inc=1, device_id=group_at(r), device_id_type=MESH)
-    for rd in range(1, n_depth):
-        pl.semaphore_signal(barrier, inc=1, device_id=depth_at(rd), device_id_type=MESH)
+    def everyone_at(r, rd):
+        there = group_at(r)
+        return (there[0], there[1], lax.rem(depth + rd, n_depth))
+
+    everyone = [(r, rd) for r in [0] + order for rd in range(n_depth) if (r, rd) != (0, 0)]
+    everyone = everyone[::-1]
+    for r, rd in everyone:
+        pl.semaphore_signal(barrier, inc=1, device_id=everyone_at(r, rd), device_id_type=MESH)
 
     row = lax.broadcasted_iota(jnp.int32, (ROWS, lanes), 0)
 
@@ -199,7 +202,7 @@
 
     lax.fori_loop(0, grains, prepare, 0)
     place_copy.wait()
-    pl.semaphore_wait(barrier, tiles - 1 + n_depth - 1)
+    pl.semaphore_wait(barrier, len(everyone))
 
     sent = []
 
@@ -353,11 +356,11 @@
     flow_keys = [("flow", 1)] if merged else [("flow", 1), ("flow", -1)]
     for key in flow_keys + [("cross", 1), ("cross", -1), ("depth", 1), ("depth", -1)]:
         sources[key] = len(sources)
-    padded_rows = -(-len(sources) * cells // 128) * 128
-
-    def columns_of(pick):
+    outer_keys = [key for key in sources if key[0] != "own"]
+
+    def columns_of(keys, pick):
         rows = []
-        for axis, side in sources:
+        for axis, side in keys:
             if axis == "own":
                 rows.append(pick(0, None))
             elif axis == "flow":
@@ -366,7 +369,7 @@
                 rows.append(pick(slot_cross[side], None))
             else:
                 rows.append(pick(None, depth_index[side]))
-        spare = padded_rows - len(sources) * cells
+        spare = -len(keys) * cells % 128
         if spare:
             rows.append(jnp.zeros((spare, lanes), jnp.float32))
         return jnp.transpose(jnp.concatenate(rows, axis=0))
@@ -416,6 +419,7 @@
     turned = [
         SCALE
         * columns_of(
+            list(sources),
             lambda slot, i, c=c: (
                 off_group[slot, c * cells : (c + 1) * cells, :]
                 if i is None
@@ -447,19 +451,18 @@
     diagonal = STIFFEN + rowsum - PER_PARTICLE
     inverse = 1.0 / diagonal
 
-    def weighted(step, j):
-        turned_field = columns_of(
-            lambda slot, i: krylov[step, j, slot] if i is None else krylov_depth[step, j, i]
-        )
+    def products(columns, base, inside):
         rows = []
         for cell in range(cells):
             total = None
             for low in range(0, lanes, 64):
                 acc = None
                 for position, (column, _) in enumerate(groups[cell]):
+                    if (column < cells) != inside:
+                        continue
                     term = (
                         weights[cell, position, low : low + 64, :]
-                        * turned_field[low : low + 64, column : column + 1]
+                        * columns[low : low + 64, column - base : column - base + 1]
                     )
                     acc = term if acc is None else acc + term
                 acc = jnp.sum(acc.reshape(8, 8, lanes), axis=0)
@@ -467,10 +470,23 @@
             rows.append(jnp.sum(total, axis=0, keepdims=True))
         return jnp.concatenate(rows, axis=0)
 
+    def inner(field):
+        return products(columns_of([("own", 0)], lambda slot, i: field), 0, True)
+
+    def outer(step, j):
+        columns = columns_of(
+            outer_keys,
+            lambda slot, i: krylov[step, j, slot] if i is None else krylov_depth[step, j, i],
+        )
+        return products(columns, cells, False)
+
     pressure = jnp.zeros((cells, lanes), jnp.float32)
     spread_before = None
     residual = None
     pressure_all = None
+    corner = lax.broadcasted_iota(
+        jnp.int32, (2 * ITERS, lanes), 0
+    ) == lax.broadcasted_iota(jnp.int32, (2 * ITERS, lanes), 1)
     for step in range(STEPS):
         if step:
             for g in range(grains):
@@ -519,46 +535,33 @@
                         group_at(r),
                     )
                 )
+            inside = inner(fields[j]) - PER_PARTICLE * fields[j]
             for copy in list(close.values()) + beside:
                 copy.wait_recv()
-            fields.append((weighted(step, j) - PER_PARTICLE * fields[j]) * inverse)
+            fields.append((inside + outer(step, j)) * inverse)
         moments = []
         for j in range(ITERS):
             scaled = diagonal * fields[j]
             moments.append(jnp.sum(scaled * fields[j], axis=0, keepdims=True))
             moments.append(jnp.sum(scaled * fields[j + 1], axis=0, keepdims=True))
-        part_group[step, 0] = jnp.concatenate(moments, axis=0)
+        own = jnp.sum(jnp.concatenate(moments, axis=0), axis=1, keepdims=True)
+        own = jnp.sum(jnp.where(corner, own, 0.0), axis=0, keepdims=True)
+        part[step, 0] = own
         waits = [
             ship(
-                part_group.at[step, 0],
-                part_group.at[step, r],
-                part_send.at[step, r],
-                part_recv.at[step, r],
-                group_at(r),
+                part.at[step, 0],
+                part.at[step, r * n_depth + rd],
+                part_send.at[step, r * n_depth + rd],
+                part_recv.at[step, r * n_depth + rd],
+                everyone_at(r, rd),
             )
-            for r in order
+            for r, rd in everyone
         ]
         for copy in waits:
             copy.wait_recv()
-        total = part_group[step, 0]
-        for r in range(1, tiles):
-            total = total + part_group[step, r]
-        part_depth[step, 0] = total
-        waits = [
-            ship(
-                part_depth.at[step, 0],
-                part_depth.at[step, rd],
-                part_send.at[step, tiles + rd],
-                part_recv.at[step, tiles + rd],
-                depth_at(rd),
-            )
-            for rd in range(1, n_depth)
-        ]
-        for copy in waits:
-            copy.wait_recv()
-        for rd in range(1, n_depth):
-            total = total + part_depth[step, rd]
-        total = jnp.broadcast_to(jnp.sum(total, axis=1, keepdims=True), total.shape)
+        total = jnp.sum(part[step], axis=0)
+        total = jnp.sum(jnp.where(corner, total, 0.0), axis=1, keepdims=True)
+        total = jnp.broadcast_to(total, (2 * ITERS, lanes))
         scalars = [total[q : q + 1, :] for q in range(2 * ITERS)]
         gram = [
             [scalars[i + j] - scalars[i + j + 1] for j in range(ITERS)] for i in range(ITERS)
@@ -654,16 +657,15 @@
             vmem((STEPS, tiles, cells, lanes), f32),
             vmem((STEPS, ITERS, tiles, cells, lanes), f32),
             vmem((STEPS, ITERS, near_count, cells, lanes), f32),
-            vmem((STEPS, tiles, 2 * ITERS, lanes), f32),
-            vmem((STEPS, n_depth, 2 * ITERS, lanes), f32),
+            vmem((STEPS, tiles * n_depth, 1, lanes), f32),
             dma((tiles + near_count,)),
             dma((tiles + near_count,)),
             dma((STEPS, tiles)),
             dma((STEPS, tiles)),
             dma((STEPS, ITERS, tiles + near_count)),
             dma((STEPS, ITERS, tiles + near_count)),
-            dma((STEPS, tiles + n_depth)),
-            dma((STEPS, tiles + n_depth)),
+            dma((STEPS, tiles * n_depth)),
+            dma((STEPS, tiles * n_depth)),
             dma,
         ],
         compiler_params=pltpu.CompilerParams(

time: 105 us -> 98.6 us (0.939)
  Pallas kernels: 102 us -> 95.9 us
    pallas_call x1, Pallas kernels: 102 us -> 95.9 us  [per_device(): pl.pallas_call(functools.partial(kernel, sizes, dims), out_shape=(jax.Sha...]
where the time goes in v2:
time: 98.6 us; the launch traced here: 98.4 us
  Pallas kernels  95.9 us (97%)
  local copies, waits for them, and re-layouts  1.88 us (2%)
    pallas_call x1, Pallas kernels, per_device(): pl.pallas_call(functools.partial(kernel, sizes, dims), out_shape=(jax.Sha...  95.9 us

profile of v2, /device:TPU:0, one launch (start us, length us, event | category | flops | bytes accessed | tf_op | source)
XLA Modules:
  0.0 98.4 jit_solution(3846648011995027826)
XLA Ops:
  0.6 95.9 %coupled.1 = (f32[16,128]{1,0:T(8,128)}, f32[3,16]{1,0:T(4,128)}) custom-call(f32[48,128]{1,0:T(8,128)} %bitcast.11, f32[16,128]{1,0:T(8,128)} %bitcast.12, f32[16,3,16,128]{3,2,1,0:T(8,128)} %bitcast.9, f32[16,3,16,128]{3,2,1,0:T(8,128)} %bitcast.10, s32[16,1,16]{2,1,0:T(1,128)} %bitcast.13, s32[16,16]{1,0:T(8,128)} %cell_ref.1, f32[3,16]{1,0:T(4,128)} %bitcast.15, ...), custom_call_target="tpu_custom_call" | custom-call | tf_op jit(solution)/shard_map/coupled/pallas_call | solution.py:627
  96.5 0.0 copy-start
  96.6 1.3 %copy.12 = f32[1,4,4,128]{3,2,1,0:T(4,128)} copy(f32[1,4,4,128]{3,2,1,0:T(4,128)} %bitcast.14) | data formatting | bytes 16384
  97.8 0.0 copy-done
  97.9 0.6 copy.13
Async XLA Ops:
  96.5 1.3 %copy-start = (f32[3,16]{1,0:T(4,128)S(1)}, f32[3,16]{1,0:T(4,128)}, u32[]{:S(2)}) copy-start(f32[3,16]{1,0:T(4,128)} %get-tuple-element.5) | copy-start | bytes 580

commit v3 on v2

--- a/solution.py
+++ b/solution.py
@@ -74,9 +74,9 @@
     off_depth,
     weights,
     own_rows,
-    own_columns,
+    own_parts,
     point_rows,
-    point_parts,
+    point_columns,
     normal_rows,
     normal_parts,
     near,
@@ -184,6 +184,7 @@
     ).astype(jnp.bfloat16)
 
     def prepare(g, carry):
+        stacked = []
         for b in range(per_grain):
             point = jnp.where(row > 3, 1.0, 0.0)
             normal = jnp.zeros((ROWS, lanes), jnp.float32)
@@ -195,7 +196,13 @@
             square = jnp.sum(jnp.where(row < 3, point * point, 0.0), axis=0, keepdims=True)
             point = jnp.where(row == 3, square, point)
             point_rows[g, b] = point
-            point_parts[g, b] = jnp.concatenate(two_parts(point), axis=0).astype(jnp.bfloat16)
+            high, rest = two_parts(point)
+            stacked += [high, rest, high, rest]
+            if b % GROUP == GROUP - 1:
+                point_columns[g * (per_grain // GROUP) + b // GROUP] = jnp.transpose(
+                    jnp.concatenate(stacked, axis=0)
+                ).astype(jnp.bfloat16)
+                stacked = []
             normal_rows[g, b] = normal
             normal_parts[g, b] = jnp.concatenate(two_parts(normal), axis=0).astype(jnp.bfloat16)
         return carry
@@ -238,22 +245,19 @@
     off_group[0] = off_ref[...]
 
     def own_pass(slot, carry):
-        for low in range(0, cells, GROUP):
-            stacked = []
-            for cell in range(low, low + GROUP):
-                base = jnp.where(row == 3, -1.0, jnp.where(row == 5, SHIFT, 0.0))
-                square = None
-                for c in range(3):
-                    spot = c * cells + cell
-                    own = SCALE * (off_group[slot, spot : spot + 1, :] - MIDDLE)
-                    base = jnp.where(row == c, 2.0 * own, base)
-                    square = own * own if square is None else square + own * own
-                base = jnp.where(row == 4, -square, base)
-                own_rows[slot * cells + cell] = base
-                high, rest = two_parts(base)
-                stacked += [high, high, rest, rest]
-            own_columns[slot * (cells // GROUP) + low // GROUP] = jnp.transpose(
-                jnp.concatenate(stacked, axis=0)
+        for cell in range(cells):
+            base = jnp.where(row == 3, -1.0, jnp.where(row == 5, SHIFT, 0.0))
+            square = None
+            for c in range(3):
+                spot = c * cells + cell
+                own = SCALE * (off_group[slot, spot : spot + 1, :] - MIDDLE)
+                base = jnp.where(row == c, 2.0 * own, base)
+                square = own * own if square is None else square + own * own
+            base = jnp.where(row == 4, -square, base)
+            own_rows[slot * cells + cell] = base
+            high, rest = two_parts(base)
+            own_parts[slot * cells + cell] = jnp.concatenate(
+                [high, high, rest, rest], axis=0
             ).astype(jnp.bfloat16)
         return carry
 
@@ -262,24 +266,20 @@
     lax.fori_loop(0, tiles, own_pass, 0)
 
     def near_pass(g, carry):
+        blank = jnp.zeros((4 * ROWS, lanes), jnp.bfloat16)
         for b in range(per_grain):
-            place = place_ref[g, b]
-            member = lax.rem(place, GROUP)
-            parts = point_parts[g, b]
-            stacked = []
-            for k in range(GROUP):
-                picked = jnp.where(member == k, parts, jnp.zeros_like(parts))
-                stacked += [picked, picked]
+            stacked = [blank] * GROUP
+            stacked[b % GROUP] = own_parts[place_ref[g, b]]
             weight = jnp.exp2(
                 jnp.dot(
-                    own_columns[lax.div(place, GROUP)],
+                    point_columns[g * (per_grain // GROUP) + b // GROUP],
                     jnp.concatenate(stacked, axis=0),
                     preferred_element_type=jnp.float32,
                 )
             )
             upper = weight.astype(jnp.bfloat16)
-            near[g * per_grain + b, :, :lanes] = upper
-            near[g * per_grain + b, :, lanes:] = (weight - upper.astype(jnp.float32)).astype(
+            near[g * per_grain + b, :lanes, :] = upper
+            near[g * per_grain + b, lanes:, :] = (weight - upper.astype(jnp.float32)).astype(
                 jnp.bfloat16
             )
         return carry
@@ -301,10 +301,9 @@
                     ).astype(jnp.bfloat16)
                 else:
                     parts = normal_parts[g, b]
-                total = lax.dot_general(
+                total = jnp.dot(
                     jnp.concatenate([parts, parts], axis=1),
                     near[g * per_grain + b],
-                    (((1,), (1,)), ((), ())),
                     preferred_element_type=jnp.float32,
                 )
                 total = total[:ROWS] + total[ROWS:]
@@ -637,12 +636,12 @@
             vmem((near_count, 3 * cells, lanes), f32),
             vmem((cells, 7, lanes, lanes), f32),
             vmem((tiles * cells, ROWS, lanes), f32),
-            vmem((tiles * cells // GROUP, lanes, 4 * ROWS * GROUP), jnp.bfloat16),
+            vmem((tiles * cells, 4 * ROWS, lanes), jnp.bfloat16),
+            vmem((grains, per_grain, ROWS, lanes), f32),
+            vmem((blocks // GROUP, lanes, 4 * ROWS * GROUP), jnp.bfloat16),
             vmem((grains, per_grain, ROWS, lanes), f32),
             vmem((grains, per_grain, 2 * ROWS, lanes), jnp.bfloat16),
-            vmem((grains, per_grain, ROWS, lanes), f32),
-            vmem((grains, per_grain, 2 * ROWS, lanes), jnp.bfloat16),
-            vmem((blocks, lanes, 2 * lanes), jnp.bfloat16),
+            vmem((blocks, 2 * lanes, lanes), jnp.bfloat16),
             vmem((grains, per_grain, ROWS, lanes), f32),
             vmem((blocks, lanes), f32),
             vmem((tiles * cells, lanes), f32),

time: 98.6 us -> 92.2 us (0.935)
  Pallas kernels: 95.9 us -> 89.5 us
    pallas_call x1, Pallas kernels: 95.9 us -> 89.5 us  [per_device(): pl.pallas_call(functools.partial(kernel, sizes, dims), out_shape=(jax.Sha...]
where the time goes in v3:
time: 92.2 us; the launch traced here: 92 us
  Pallas kernels  89.5 us (97%)
  local copies, waits for them, and re-layouts  1.88 us (2%)
    pallas_call x1, Pallas kernels, per_device(): pl.pallas_call(functools.partial(kernel, sizes, dims), out_shape=(jax.Sha...  89.5 us
    unnamed x4, local copies, waits for them, and re-layouts  1.88 us

profile of v3, /device:TPU:0, one launch (start us, length us, event | category | flops | bytes accessed | tf_op | source)
XLA Modules:
  0.0 92.0 jit_solution(455174052563241309)
XLA Ops:
  0.6 89.5 %coupled.1 = (f32[16,128]{1,0:T(8,128)}, f32[3,16]{1,0:T(4,128)}) custom-call(f32[48,128]{1,0:T(8,128)} %bitcast.11, f32[16,128]{1,0:T(8,128)} %bitcast.12, f32[16,3,16,128]{3,2,1,0:T(8,128)} %bitcast.9, f32[16,3,16,128]{3,2,1,0:T(8,128)} %bitcast.10, s32[16,1,16]{2,1,0:T(1,128)} %bitcast.13, s32[16,16]{1,0:T(8,128)} %cell_ref.1, f32[3,16]{1,0:T(4,128)} %bitcast.15, ...), custom_call_target="tpu_custom_call" | custom-call | tf_op jit(solution)/shard_map/coupled/pallas_call | solution.py:626
  90.1 0.0 copy-start
  90.1 1.3 %copy.12 = f32[1,4,4,128]{3,2,1,0:T(4,128)} copy(f32[1,4,4,128]{3,2,1,0:T(4,128)} %bitcast.14) | data formatting | bytes 16384
  91.4 0.0 copy-done
  91.4 0.6 copy.13
Async XLA Ops:
  90.1 1.3 %copy-start = (f32[3,16]{1,0:T(4,128)S(1)}, f32[3,16]{1,0:T(4,128)}, u32[]{:S(2)}) copy-start(f32[3,16]{1,0:T(4,128)} %get-tuple-element.5) | copy-start | bytes 580

commit v4 on v3

--- a/solution.py
+++ b/solution.py
@@ -18,6 +18,7 @@
 MESH = pl.DeviceIdType.MESH
 ROWS = 8
 GROUP = 4
+FOLDED = 4
 MIDDLE = 0.5
 
 
@@ -104,6 +105,10 @@
     part_send,
     part_recv,
     place_sem,
+    press_away,
+    press_home,
+    press_send,
+    press_recv,
 ):
     n_flow, n_cross, n_depth = sizes
     size_x, size_y, size_z = dims
@@ -113,17 +118,34 @@
     blocks = grains * per_grain
     flow, cross, depth = (lax.axis_index("flow"), lax.axis_index("cross"), lax.axis_index("depth"))
 
+    fold = n_cross == FOLDED
+
+    def folded(place):
+        if not fold:
+            return place
+        return place + lax.div(place, 2) * (2 * n_cross - 3 - 2 * place)
+
+    line = folded(cross)
+
+    def home_at(slot):
+        rf, rc = divmod(slot, n_cross)
+        return (lax.rem(flow + rf, n_flow), lax.rem(cross + rc, n_cross), depth)
+
     def group_at(slot):
         rf, rc = divmod(slot, n_cross)
-        return (lax.rem(flow + rf, n_flow), lax.rem(cross + rc, n_cross), depth)
+        return (lax.rem(flow + rf, n_flow), folded(lax.rem(line + rc, n_cross)), depth)
 
     def group_back(slot):
         rf, rc = divmod(slot, n_cross)
         return (
             lax.rem(flow + n_flow - rf, n_flow),
-            lax.rem(cross + n_cross - rc, n_cross),
+            folded(lax.rem(line + n_cross - rc, n_cross)),
             depth,
         )
+
+    def tile_at(slot):
+        there = lax.rem(flow + n_flow - lax.div(slot, n_cross), n_flow)
+        return there * n_cross + lax.rem(line + n_cross - lax.rem(slot, n_cross), n_cross)
 
     def depth_at(rd):
         return (flow, cross, lax.rem(depth + rd, n_depth))
@@ -151,7 +173,7 @@
 
     tile = tile_ref[:, 0, :]
     slot_flow_of = lax.rem(flow + n_flow - lax.div(tile, n_cross), n_flow)
-    slot_cross_of = lax.rem(cross + n_cross - lax.rem(tile, n_cross), n_cross)
+    slot_cross_of = lax.rem(line + n_cross - lax.rem(tile, n_cross), n_cross)
     slot_of = slot_flow_of * n_cross + slot_cross_of
     place_rows[...] = jnp.zeros(place_rows.shape, jnp.int32)
     place_rows[:, :per_grain] = slot_of * cells + cell_ref[...]
@@ -226,10 +248,11 @@
         sent.append(copy)
         return copy
 
+    home = flow * n_cross + cross
     off_copies = {}
     for r in order:
         off_copies[r] = ship(
-            off_ref, off_group.at[r], off_send.at[r], off_recv.at[r], group_at(r)
+            off_ref, off_group.at[home], off_send.at[r], off_recv.at[r], home_at(r)
         )
     off_depth_copies = []
     for i, rd in enumerate(near_depth):
@@ -239,18 +262,19 @@
                 off_depth.at[i],
                 off_send.at[tiles + i],
                 off_recv.at[tiles + i],
-                depth_at(rd),
+                (flow, line, lax.rem(depth + rd, n_depth)),
             )
         )
-    off_group[0] = off_ref[...]
+    off_group[home] = off_ref[...]
 
     def own_pass(slot, carry):
+        tile_of = tile_at(slot)
         for cell in range(cells):
             base = jnp.where(row == 3, -1.0, jnp.where(row == 5, SHIFT, 0.0))
             square = None
             for c in range(3):
                 spot = c * cells + cell
-                own = SCALE * (off_group[slot, spot : spot + 1, :] - MIDDLE)
+                own = SCALE * (off_group[tile_of, spot : spot + 1, :] - MIDDLE)
                 base = jnp.where(row == c, 2.0 * own, base)
                 square = own * own if square is None else square + own * own
             base = jnp.where(row == 4, -square, base)
@@ -331,6 +355,8 @@
         )
         spread = spread[:, :lanes] + spread[:, lanes:]
         give[step] = spread.reshape(tiles, cells, lanes)
+        own_slot = lax.rem(line + n_cross - cross, n_cross)
+        give[step, own_slot] = give[step, own_slot] + source_ref[...]
         return [
             ship(
                 give.at[step, r],
@@ -420,17 +446,18 @@
         * columns_of(
             list(sources),
             lambda slot, i, c=c: (
-                off_group[slot, c * cells : (c + 1) * cells, :]
+                off_group[tile_at(slot), c * cells : (c + 1) * cells, :]
                 if i is None
                 else off_depth[i, c * cells : (c + 1) * cells, :]
             )
         )
         for c in range(3)
     ]
+    mine = tile_at(0)
     sum_rows = []
     for cell in range(cells):
         own = [
-            SCALE * off_ref[c * cells + cell : c * cells + cell + 1, :] for c in range(3)
+            SCALE * off_group[mine, c * cells + cell : c * cells + cell + 1, :] for c in range(3)
         ]
         full = None
         for position, (column, steps) in enumerate(groups[cell]):
@@ -479,6 +506,16 @@
         )
         return products(columns, cells, False)
 
+    def return_copy():
+        return pltpu.make_async_remote_copy(
+            src_ref=press_away,
+            dst_ref=press_home,
+            send_sem=press_send,
+            recv_sem=press_recv,
+            device_id=(flow, line, depth),
+            device_id_type=MESH,
+        )
+
     pressure = jnp.zeros((cells, lanes), jnp.float32)
     spread_before = None
     residual = None
@@ -497,7 +534,7 @@
             copies = to_fluid(step)
         spread = collect(step, copies)
         if step == 0:
-            residual = source_ref[...] + spread
+            residual = spread
         else:
             residual = residual + (spread - spread_before)
         spread_before = spread
@@ -574,6 +611,15 @@
         for j in range(ITERS):
             term = factors[j] * krylov[step, j].reshape(tiles * cells, lanes)
             pressure_all = term if pressure_all is None else pressure_all + term
+        if step == STEPS - 1:
+            press_out[...] = pressure
+        if fold and step == STEPS - 1:
+            press_away[...] = pressure
+
+            @pl.when(line != cross)
+            def _():
+                return_copy().start()
+
         felt_rows[...] = pressure_all
 
         def push(g, carry):
@@ -591,7 +637,13 @@
             return carry
 
         lax.fori_loop(0, grains, push, 0)
-    press_out[...] = pressure
+    if fold:
+
+        @pl.when(line != cross)
+        def _():
+            return_copy().wait()
+            press_out[...] = press_home[...]
+
     lane = lax.broadcasted_iota(jnp.int32, (ROWS, lanes), 1)
     speed = jnp.zeros((ROWS, lanes), jnp.float32)
     for g in range(grains):
@@ -666,6 +718,10 @@
             dma((STEPS, tiles * n_depth)),
             dma((STEPS, tiles * n_depth)),
             dma,
+            vmem((cells, lanes), f32),
+            vmem((cells, lanes), f32),
+            dma,
+            dma,
         ],
         compiler_params=pltpu.CompilerParams(
             collective_id=0, has_side_effects=True, vmem_limit_bytes=60 * 1024 * 1024

time: 92.2 us -> 88.8 us (0.963)
  Pallas kernels: 89.5 us -> 86.1 us
    pallas_call x1, Pallas kernels: 89.5 us -> 86.1 us  [per_device(): pl.pallas_call(functools.partial(kernel, sizes, dims), out_shape=(jax.Sha...]
where the time goes in v4:
time: 88.8 us; the launch traced here: 88.7 us
  Pallas kernels  86.1 us (97%)
  local copies, waits for them, and re-layouts  1.88 us (2%)
    pallas_call x1, Pallas kernels, per_device(): pl.pallas_call(functools.partial(kernel, sizes, dims), out_shape=(jax.Sha...  86.1 us
    unnamed x4, local copies, waits for them, and re-layouts  1.88 us

profile of v4, /device:TPU:0, one launch (start us, length us, event | category | flops | bytes accessed | tf_op | source)
XLA Modules:
  0.0 88.7 jit_solution(5806373301732339074)
XLA Ops:
  0.6 86.1 %coupled.1 = (f32[16,128]{1,0:T(8,128)}, f32[3,16]{1,0:T(4,128)}) custom-call(f32[48,128]{1,0:T(8,128)} %bitcast.11, f32[16,128]{1,0:T(8,128)} %bitcast.12, f32[16,3,16,128]{3,2,1,0:T(8,128)} %bitcast.9, f32[16,3,16,128]{3,2,1,0:T(8,128)} %bitcast.10, s32[16,1,16]{2,1,0:T(1,128)} %bitcast.13, s32[16,16]{1,0:T(8,128)} %cell_ref.1, f32[3,16]{1,0:T(4,128)} %bitcast.15, ...), custom_call_target="tpu_custom_call" | custom-call | tf_op jit(solution)/shard_map/coupled/pallas_call | solution.py:678
  86.8 0.0 copy-start
  86.8 1.3 %copy.12 = f32[1,4,4,128]{3,2,1,0:T(4,128)} copy(f32[1,4,4,128]{3,2,1,0:T(4,128)} %bitcast.14) | data formatting | bytes 16384
  88.1 0.0 copy-done
  88.1 0.6 copy.13
Async XLA Ops:
  86.8 1.3 %copy-start = (f32[3,16]{1,0:T(4,128)S(1)}, f32[3,16]{1,0:T(4,128)}, u32[]{:S(2)}) copy-start(f32[3,16]{1,0:T(4,128)} %get-tuple-element.5) | copy-start | bytes 580
